TPU v7x, 128 devices: a whole 4x4x4 slice. The times are simulated.
128 devices in a mesh: row: 8 (over y, core), col: 16 (over z, x).
Axes of the slice: x: 4, y: 4, z: 4, core: 2. Of those that a mesh axis runs over, the one named last changes fastest.
Arguments:
- points: float32 [3, 262144], P(None, ('row', 'col')), as said below
- values: float32 [16, 262144], P(None, ('row', 'col'))
- tile_lists: int32 [3, 6144], P(None, ('row', 'col')), may hold values from 0 to 127, as said below
Outputs:
- solution: float32 [16, 262144], P(None, ('row', 'col'))
- residual: float32 [16, 262144], P(None, ('row', 'col'))
Inputs may be any that keep to these rules, and one draw needn't show every extreme that they name: `tile_lists`: on every device the live slots come first and the rest hold 0, 0, 0; a device holds at most 48 live slots and some device holds exactly that many; no unordered pair of blocks is listed twice, in either order. Block pairs whose points can come within the support radius are listed. Coordinates of point blocks that lie in cells of a square lattice of unit cells, 256 points to a block.
All inputs are finite; a program needn't handle non-finite values.
Results may differ from a plain program's by a relative error of at most 0.0003.
Values sent between devices are 32-bit elements; how exact they have to be, the bound alone decides.
A program may use at most 64 MiB of HBM per device.

v0:
```python
import jax
import jax.numpy as jnp
from jax import lax
from jax.sharding import PartitionSpec as P

BLK = 256
ITERS = 2
support = 0.5
ridge_shift = 1.0
group_width = 12


def wendland(left, right):
    offsets = left[:, :, :, None] - right[:, :, None, :]
    distance = jnp.sqrt(jnp.sum(offsets * offsets, axis=0))
    scaled = distance / support
    remain = jnp.maximum(1.0 - scaled, 0.0)
    return remain * remain * remain * remain * (4.0 * scaled + 1.0)


def local(points, values, tile_lists):
    fields, owned_points = values.shape
    per_device = owned_points // BLK
    col_count = lax.axis_size("col")
    row_count = lax.axis_size("row")
    row_id = lax.axis_index("row")
    col_id = lax.axis_index("col")
    row_span = col_count * per_device
    col_span = row_count * per_device
    cloud_rows = lax.all_gather(points, "col", axis=1, tiled=True).reshape(3, row_span, BLK)
    cloud_cols = lax.all_gather(points, "row", axis=1, tiled=True).reshape(3, col_span, BLK)
    row_local = tile_lists[0]
    col_local = tile_lists[1]
    row_block = row_id * row_span + row_local
    col_block = (col_local // per_device * col_count + col_id) * per_device + col_local % per_device
    weight = tile_lists[2].astype(jnp.float32)
    mirror_weight = weight * (row_block != col_block).astype(jnp.float32)
    group_count = tile_lists.shape[1] // group_width
    group_shape = (group_count, group_width)
    groups = (
        row_local.reshape(group_shape),
        col_local.reshape(group_shape),
        weight.reshape(group_shape),
        mirror_weight.reshape(group_shape),
    )

    def accumulate(totals, member_set, along_rows, along_cols):
        forward_total, behind_total = totals
        row_index, col_index, row_weight, col_weight = member_set
        kernel = wendland(cloud_rows[:, row_index], cloud_cols[:, col_index])
        forward = jnp.einsum(
            "gxy,fgy->fgx", kernel, along_cols[:, col_index], precision=lax.Precision.HIGHEST
        )
        behind = jnp.einsum(
            "gxy,fgx->fgy", kernel, along_rows[:, row_index], precision=lax.Precision.HIGHEST
        )
        forward_total = forward_total.at[:, row_index].add(forward * row_weight[None, :, None])
        behind_total = behind_total.at[:, col_index].add(behind * col_weight[None, :, None])
        return (forward_total, behind_total)

    def squares(vector):
        return lax.psum(jnp.sum(vector * vector, axis=1), ("row", "col"))

    solution = jnp.zeros_like(values)
    residual = values
    direction = values
    norm_now = squares(residual)
    for iteration in range(ITERS):
        operate_along_rows = lax.all_gather(direction, "col", axis=1, tiled=True).reshape(
            fields, row_span, BLK
        )
        operate_along_cols = lax.all_gather(direction, "row", axis=1, tiled=True).reshape(
            fields, col_span, BLK
        )
        initial = (
            jnp.zeros((fields, row_span, BLK), jnp.float32),
            jnp.zeros((fields, col_span, BLK), jnp.float32),
        )

        def visit_all(totals, member_set):
            return (accumulate(totals, member_set, operate_along_rows, operate_along_cols), None)

        (operate_forward_total, operate_behind_total), _ = lax.scan(visit_all, initial, groups)
        mine_forward = lax.psum_scatter(
            operate_forward_total.reshape(fields, row_span * BLK),
            "col",
            scatter_dimension=1,
            tiled=True,
        )
        mine_behind = lax.psum_scatter(
            operate_behind_total.reshape(fields, col_span * BLK),
            "row",
            scatter_dimension=1,
            tiled=True,
        )
        applied = ridge_shift * direction + mine_forward + mine_behind
        curve_sum = lax.psum(jnp.sum(direction * applied, axis=1), ("row", "col"))
        step_length = norm_now / curve_sum
        solution = solution + step_length[:, None] * direction
        residual = residual - step_length[:, None] * applied
        norm_next = squares(residual)
        direction = residual + (norm_next / norm_now)[:, None] * direction
        norm_now = norm_next
    return (solution, residual)


def solution(mesh):
    placed = (P(None, ("row", "col")), P(None, ("row", "col")), P(None, ("row", "col")))
    return jax.shard_map(
        local,
        mesh=mesh,
        in_specs=placed,
        out_specs=(P(None, ("row", "col")), P(None, ("row", "col"))),
        check_vma=False,
    )
```

profile of v0, /device:TPU:1, one launch (start us, length us, event | category | flops | bytes accessed | tf_op | source)
XLA Modules:
  0.0 775.9 jit_solution(17273977491042123347)
XLA Ops:
  11.6 16.0 %all_gather.20 = f32[3,16384]{1,0:T(4,128)} all-gather(f32[3,2048]{1,0:T(4,128)} %param.7), channel_id=1, replica_groups=mesh['row'=8,'col'=16] {'row'}, dimensions={1}, use_global_device_ids=true | all-gather | bytes 221184 | tf_op jit(solution)/shard_map/all_gather | solution.py:31
  27.5 23.3 %all_gather.19 = f32[3,32768]{1,0:T(4,128)} all-gather(f32[3,2048]{1,0:T(4,128)} %param.7), channel_id=1, replica_groups=mesh['row'=8,'col'=16] {'col'}, dimensions={1}, use_global_device_ids=true | all-gather | bytes 417792 | tf_op jit(solution)/shard_map/all_gather | solution.py:30
  54.5 27.5 %all-gather.7.cloned.1.call-done = f32[16,32768]{1,0:T(8,128)} async-done(((f32[16,2048]{1,0:T(8,128)}), f32[16,32768]{1,0:T(8,128)}) %all-gather.7.cloned.1.call-update) | async-done | bytes 2097168 | tf_op jit(solution)/shard_map/all_gather | solution.py:69
  82.0 3.3 copy.60
  85.6 96.3 %while.28 = (s32[]{:T(128)}, f32[16,128,256]{2,0,1:T(8,128)S(1)}, f32[16,64,256]{2,0,1:T(8,128)S(1)}, s32[4,12]{1,0:T(4,128)}, s32[4,12]{1,0:T(4,128)S(1)}, /*in...) while((s32[]{:T(128)}, f32[16,128,256]{2,0,1:T(8,128)S(1)}, ...), condition=%wide.region_6.7_spmd, body=%wide.region_2.6_spmd.sunk | while | flops 322635840 | bytes 12567965 | solution.py:83
  98.8 3.9 fusion.85
  102.7 4.1 fusion.84
  122.9 3.9 fusion.85
  126.8 4.1 fusion.84
  146.9 3.9 fusion.85
  150.8 4.1 fusion.84
  171.0 3.9 fusion.85
  174.9 4.1 fusion.84
  184.7 28.9 %reduce-scatter.7.cloned.1.call-done = f32[16,2048]{1,0:T(8,128)} async-done(((f32[16,16384]{1,0:T(8,128)}), f32[16,2048]{1,0:T(8,128)}) %reduce-scatter.7.cloned.1.call-update) | async-done | bytes 131088 | tf_op jit(solution)/shard_map/reduce_scatter | solution.py:90
  213.6 78.3 %reduce-scatter.5.cloned.1.call-done = f32[16,2048]{1,0:T(8,128)} async-done(((f32[16,32768]{1,0:T(8,128)}), f32[16,2048]{1,0:T(8,128)}) %reduce-scatter.5.cloned.1.call-update) | async-done | bytes 131088 | tf_op jit(solution)/shard_map/reduce_scatter | solution.py:84
  293.1 66.1 %all-reduce = (f32[16]{0:T(128)S(1)}, f32[16]{0:T(128)S(1)}) all-reduce(f32[16]{0:T(128)S(1)} %get-tuple-element.338, f32[16]{0:T(128)S(1)} %get-tuple-element.337), channel_id=1, replica_groups=mesh['row'=8,'col'=16] {'row','col'}, use_global_device_ids=true, to_apply=%region_1.2 | all-reduce | flops 32 | bytes 256 | tf_op jit(solution)/shard_map/psum | solution.py:62
  360.3 62.5 %psum.30 = f32[16]{0:T(128)S(1)} all-reduce(f32[16]{0:T(128)S(1)} %get-tuple-element.387), channel_id=1, replica_groups=mesh['row'=8,'col'=16] {'row','col'}, use_global_device_ids=true, to_apply=%region_12.13 | all-reduce | flops 16 | bytes 128 | tf_op jit(solution)/shard_map/psum | solution.py:62
  424.2 20.3 %all-gather.9.cloned.1.call-done = f32[16,16384]{1,0:T(8,128)} async-done(((f32[16,2048]{1,0:T(8,128)}), f32[16,16384]{1,0:T(8,128)}) %all-gather.9.cloned.1.call-update) | async-done | bytes 1048592 | tf_op jit(solution)/shard_map/all_gather | solution.py:72
  446.8 43.3 %all-gather.11.cloned.1.call-done = f32[16,32768]{1,0:T(8,128)} async-done(((f32[16,2048]{1,0:T(8,128)}), f32[16,32768]{1,0:T(8,128)}) %all-gather.11.cloned.1.call-update) | async-done | bytes 2097168 | tf_op jit(solution)/shard_map/all_gather | solution.py:69
  490.2 3.3 copy.59
  493.8 96.3 %while.29 = (s32[]{:T(128)}, f32[16,128,256]{2,0,1:T(8,128)S(1)}, f32[16,64,256]{2,0,1:T(8,128)S(1)}, s32[4,12]{1,0:T(4,128)}, s32[4,12]{1,0:T(4,128)S(1)}, /*in...) while((s32[]{:T(128)}, f32[16,128,256]{2,0,1:T(8,128)S(1)}, ...), condition=%wide.region_17.18_spmd, body=%wide.region_13.17_spmd.sunk | while | flops 322635840 | bytes 12567965 | solution.py:83
  507.0 3.9 fusion.93
  510.9 4.1 fusion.92
  531.0 3.9 fusion.93
  534.9 4.1 fusion.92
  555.1 3.9 fusion.93
  559.0 4.1 fusion.92
  579.2 3.9 fusion.93
  583.1 4.1 fusion.92
  592.9 28.9 %reduce-scatter.11.cloned.1.call-done = f32[16,2048]{1,0:T(8,128)} async-done(((f32[16,16384]{1,0:T(8,128)}), f32[16,2048]{1,0:T(8,128)}) %reduce-scatter.11.cloned.1.call-update) | async-done | bytes 131088 | tf_op jit(solution)/shard_map/reduce_scatter | solution.py:90
  621.8 78.5 %reduce-scatter.9.cloned.1.call-done = f32[16,2048]{1,0:T(8,128)} async-done(((f32[16,32768]{1,0:T(8,128)}), f32[16,2048]{1,0:T(8,128)}) %reduce-scatter.9.cloned.1.call-update) | async-done | bytes 131088 | tf_op jit(solution)/shard_map/reduce_scatter | solution.py:84
  701.3 65.9 %psum.31 = f32[16]{0:T(128)S(1)} all-reduce(f32[16]{0:T(128)S(1)} %multiply_reduce_fusion.2), channel_id=1, replica_groups=mesh['row'=8,'col'=16] {'row','col'}, use_global_device_ids=true, to_apply=%region_21.22 | all-reduce | flops 16 | bytes 128 | tf_op jit(solution)/shard_map/psum | solution.py:97
  (195 shorter events, 151.3 us)
Async XLA Ops:
  7.2 45.0 %all-gather.5.cloned.1.call-start = ((), (), s32[]{:S(2)}) async-start(), calls=%async_computation.4 | async-start | bytes 1179648 | tf_op jit(solution)/shard_map/all_gather | solution.py:72
  7.9 74.1 %all-gather.7.cloned.1.call-start = ((), (), s32[]{:S(2)}) async-start(), calls=%async_computation.5 | async-start | bytes 2228224 | tf_op jit(solution)/shard_map/all_gather | solution.py:69
  8.6 205.0 %reduce-scatter.7.cloned.1.call-start = ((), (), s32[]{:S(2)}) async-start(), calls=%async_computation.7 | async-start | bytes 1179648 | tf_op jit(solution)/shard_map/reduce_scatter | solution.py:90
  96.0 2.8 copy-start.7
  98.8 3.9 copy-start.5
  120.1 2.8 copy-start.7
  122.9 3.9 copy-start.5
  144.1 2.8 copy-start.7
  146.9 3.9 copy-start.5
  168.2 2.8 copy-start.7
  171.0 3.9 copy-start.5
  183.1 108.9 %reduce-scatter.5.cloned.1.call-start = ((), (), s32[]{:S(2)}) async-start(), calls=%async_computation.6 | async-start | bytes 2228224 | tf_op jit(solution)/shard_map/reduce_scatter | solution.py:84
  183.1 108.8 %copy-start = (f32[16,2048]{1,0:T(8,128)S(1)}, f32[16,2048]{1,0:T(8,128)}, u32[]{:S(2)}) copy-start(f32[16,2048]{1,0:T(8,128)} %param.8) | copy-start | bytes 393220
  184.7 259.8 %all-gather.9.cloned.1.call-start = ((), (), s32[]{:S(2)}) async-start(), calls=%async_computation.8 | async-start | bytes 1179648 | tf_op jit(solution)/shard_map/all_gather | solution.py:72
  359.2 134.3 %copy-start.9 = (f32[16]{0:T(128)}, f32[16]{0:T(128)S(1)}, u32[]{:S(2)}) copy-start(f32[16]{0:T(128)S(1)} %div.31) | copy-start | bytes 196
  360.3 133.1 %copy-start.3 = (f32[16,2048]{1,0:T(8,128)}, f32[16,2048]{1,0:T(8,128)S(1)}, u32[]{:S(2)}) copy-start(f32[16,2048]{1,0:T(8,128)S(1)} %get-tuple-element.388) | copy-start | bytes 393220
  422.8 70.6 %copy-start.11 = (f32[16]{0:T(128)}, f32[16]{0:T(128)S(1)}, u32[]{:S(2)}) copy-start(f32[16]{0:T(128)S(1)} %psum.30) | copy-start | bytes 196
  423.6 66.5 %all-gather.11.cloned.1.call-start = ((), (), s32[]{:S(2)}) async-start(), calls=%async_computation.9 | async-start | bytes 2228224 | tf_op jit(solution)/shard_map/all_gather | solution.py:69
  424.2 197.6 %reduce-scatter.11.cloned.1.call-start = ((), (), s32[]{:S(2)}) async-start(), calls=%async_computation.11 | async-start | bytes 1179648 | tf_op jit(solution)/shard_map/reduce_scatter | solution.py:90
  504.1 2.8 copy-start.8
  507.0 3.9 copy-start.6
  528.2 2.8 copy-start.8
  531.0 3.9 copy-start.6
  552.3 2.8 copy-start.8
  555.1 3.9 copy-start.6
  579.2 3.9 copy-start.6
  591.2 109.0 %reduce-scatter.9.cloned.1.call-start = ((), (), s32[]{:S(2)}) async-start(), calls=%async_computation.10 | async-start | bytes 2228224 | tf_op jit(solution)/shard_map/reduce_scatter | solution.py:84
  591.3 109.0 %copy-start.2 = (f32[16,2048]{1,0:T(8,128)S(1)}, f32[16,2048]{1,0:T(8,128)}, u32[]{:S(2)}) copy-start(f32[16,2048]{1,0:T(8,128)} %multiply_add_fusion.1) | copy-start | bytes 393220
  591.3 176.0 %copy-start.12 = (f32[16]{0:T(128)S(1)}, f32[16]{0:T(128)}, u32[]{:S(2)}) copy-start(f32[16]{0:T(128)} %copy-done.11) | copy-start | bytes 196
  591.3 176.0 %copy-start.1 = (f32[16,2048]{1,0:T(8,128)S(1)}, f32[16,2048]{1,0:T(8,128)}, u32[]{:S(2)}) copy-start(f32[16,2048]{1,0:T(8,128)} %param.8) | copy-start | bytes 393220
  591.3 176.0 %copy-start.4 = (f32[16,2048]{1,0:T(8,128)S(1)}, f32[16,2048]{1,0:T(8,128)}, u32[]{:S(2)}) copy-start(f32[16,2048]{1,0:T(8,128)} %copy-done.3) | copy-start | bytes 393220
  591.3 176.0 %copy-start.10 = (f32[16]{0:T(128)S(1)}, f32[16]{0:T(128)}, u32[]{:S(2)}) copy-start(f32[16]{0:T(128)} %copy-done.9) | copy-start | bytes 196
  (1 other events, 2.8 us)
Sparse Core Ops, SparseCore 0:
  9.7 26.8 all-gather.4
  38.7 43.2 all-gather.6
  183.2 30.3 reduce-scatter.6
  216.8 75.1 reduce-scatter.4
  423.7 20.7 all-gather.8
  447.1 43.0 all-gather.10
  591.3 30.3 reduce-scatter.10
  625.0 75.1 reduce-scatter.8
where the time goes:
time: 779 us; the launch traced here: 776 us
  waiting for transfers between devices  308 us (40%)
  blocking collectives  234 us (30%)
  local copies, waits for them, and re-layouts  96.2 us (12%)
  matrix products  63.5 us (8%)
  other arithmetic  59.3 us (8%)
  between operations  14.3 us (2%)
    reduce_scatter x2, waiting for transfers between devices, local(): lax.psum_scatter(operate_forward_total.reshape(fields, row_span * BLK), '...  157 us
    psum x2, blocking collectives, squares(): return lax.psum(jnp.sum(vector * vector, axis=1), ('row', 'col'))  129 us
    all_gather x2, waiting for transfers between devices, local(): lax.all_gather(direction, 'col', axis=1, tiled=True)  70.8 us
    psum x1, blocking collectives, local(): curve_sum = lax.psum(jnp.sum(direction * applied, axis=1), ('row', 'col'))  65.9 us
    reduce_scatter x2, waiting for transfers between devices, local(): lax.psum_scatter(operate_behind_total.reshape(fields, col_span * BLK), 'r...  57.8 us
    gather x32, local copies, waits for them, and re-layouts, accumulate(): kernel = wendland(cloud_rows[:, row_index], cloud_cols[:, col_index])  35.2 us
    dot_general x8, matrix products, accumulate(): jnp.einsum('gxy,fgy->fgx', kernel, along_cols[:, col_index], precision=la...  32.4 us
    dot_general x8, matrix products, accumulate(): jnp.einsum('gxy,fgx->fgy', kernel, along_rows[:, row_index], precision=la...  31.1 us
  transfers between devices with their start and end apart: 8, of which 7 were waited for; matrix products, arithmetic and copies ran while one was open for 2% of the time, Pallas kernels for 0%

commit v1 on v0

--- a/solution.py
+++ b/solution.py
@@ -66,9 +66,9 @@
     direction = values
     norm_now = squares(residual)
     for iteration in range(ITERS):
-        operate_along_rows = lax.all_gather(direction, "col", axis=1, tiled=True).reshape(
-            fields, row_span, BLK
-        )
+        operate_along_rows = jnp.concatenate(
+            lax.all_to_all(jnp.stack([direction] * lax.axis_size("col")), "col", 0, 0), axis=1
+        ).reshape(fields, row_span, BLK)
         operate_along_cols = lax.all_gather(direction, "row", axis=1, tiled=True).reshape(
             fields, col_span, BLK
         )

time: 779 us -> 740 us (0.950)
  waiting for transfers between devices: 308 us -> 244 us
  starting transfers between devices: 0.32 us -> 13 us
  local copies, waits for them, and re-layouts: 96.2 us -> 107 us
    all_gather x2 -> x0, waiting for transfers between devices: 70.8 us -> none  [local(): lax.all_gather(direction, 'col', axis=1, tiled=True)]
    all_to_all x0 -> x2, starting transfers between devices: none -> 12.8 us  [local(): lax.all_to_all(jnp.stack([direction] * lax.axis_size('col')), 'col', 0, 0)]
  transfers between devices with their start and end apart: 8 -> 8, of which waited for: 7 -> 6; matrix products, arithmetic and copies ran while one was open for 2% -> 1% of each run, Pallas kernels for 0% -> 0%
where the time goes in v1:
time: 740 us; the launch traced here: 737 us
  waiting for transfers between devices  244 us (33%)
  blocking collectives  236 us (32%)
  local copies, waits for them, and re-layouts  107 us (14%)
  matrix products  63.5 us (9%)
  other arithmetic  57.9 us (8%)
  between operations  14.3 us (2%)
  starting transfers between devices  13 us (2%)
    reduce_scatter x2, waiting for transfers between devices, local(): lax.psum_scatter(operate_forward_total.reshape(fields, row_span * BLK), '...  157 us
    psum x2, blocking collectives, squares(): return lax.psum(jnp.sum(vector * vector, axis=1), ('row', 'col'))  129 us
    psum x1, blocking collectives, local(): curve_sum = lax.psum(jnp.sum(direction * applied, axis=1), ('row', 'col'))  65.9 us
    reduce_scatter x2, waiting for transfers between devices, local(): lax.psum_scatter(operate_behind_total.reshape(fields, col_span * BLK), 'r...  58.3 us
    gather x32, local copies, waits for them, and re-layouts, accumulate(): kernel = wendland(cloud_rows[:, row_index], cloud_cols[:, col_index])  35.2 us
    dot_general x8, matrix products, accumulate(): jnp.einsum('gxy,fgy->fgx', kernel, along_cols[:, col_index], precision=la...  32.4 us
    dot_general x8, matrix products, accumulate(): jnp.einsum('gxy,fgx->fgy', kernel, along_rows[:, row_index], precision=la...  31.1 us
    all_gather x2, waiting for transfers between devices, local(): lax.all_gather(direction, 'row', axis=1, tiled=True)  26.2 us
  transfers between devices with their start and end apart: 8, of which 6 were waited for; matrix products, arithmetic and copies ran while one was open for 1% of the time, Pallas kernels for 0%

profile of v1, /device:TPU:1, one launch (start us, length us, event | category | flops | bytes accessed | tf_op | source)
XLA Modules:
  0.0 736.8 jit_solution(7644636011493723863)
XLA Ops:
  9.7 8.4 %all-to-all-start = ((f32[16,16,2048]{2,1,0:T(8,128)}), f32[16,16,2048]{2,1,0:T(8,128)S(1)}, u32[]{:S(2)}, u32[]{:S(2)}) async-start(f32[16,16,2048]{2,1,0:T(8,128)} %stack.4), calls=%async_computation | async-start | bytes 4194304 | tf_op jit(solution)/shard_map/all_to_all | solution.py:70
  20.4 15.2 %all_gather.14 = f32[3,16384]{1,0:T(4,128)} all-gather(f32[3,2048]{1,0:T(4,128)S(1)} %copy-done.6), channel_id=1, replica_groups=mesh['row'=8,'col'=16] {'row'}, dimensions={1}, use_global_device_ids=true | all-gather | bytes 221184 | tf_op jit(solution)/shard_map/all_gather | solution.py:31
  35.6 25.8 %all_gather.13 = f32[3,32768]{1,0:T(4,128)} all-gather(f32[3,2048]{1,0:T(4,128)S(1)} %copy-done.6), channel_id=1, replica_groups=mesh['row'=8,'col'=16] {'col'}, dimensions={1}, use_global_device_ids=true | all-gather | bytes 417792 | tf_op jit(solution)/shard_map/all_gather | solution.py:30
  72.3 96.3 %while.28 = (s32[]{:T(128)}, f32[16,128,256]{2,0,1:T(8,128)S(1)}, f32[16,64,256]{2,0,1:T(8,128)S(1)}, s32[4,12]{1,0:T(4,128)}, s32[4,12]{1,0:T(4,128)S(1)}, /*in...) while((s32[]{:T(128)}, f32[16,128,256]{2,0,1:T(8,128)S(1)}, ...), condition=%wide.region_6.7_spmd, body=%wide.region_2.6_spmd.sunk | while | flops 322635840 | bytes 12567965 | solution.py:83
  85.5 3.9 fusion.85
  89.4 4.1 fusion.84
  109.5 3.9 fusion.85
  113.4 4.1 fusion.84
  133.6 3.9 fusion.85
  137.5 4.1 fusion.84
  157.7 3.9 fusion.85
  161.6 4.1 fusion.84
  171.3 32.6 %reduce-scatter.7.cloned.1.call-done = f32[16,2048]{1,0:T(8,128)} async-done(((f32[16,16384]{1,0:T(8,128)}), f32[16,2048]{1,0:T(8,128)}) %reduce-scatter.7.cloned.1.call-update) | async-done | bytes 131088 | tf_op jit(solution)/shard_map/reduce_scatter | solution.py:90
  203.9 78.4 %reduce-scatter.5.cloned.1.call-done = f32[16,2048]{1,0:T(8,128)} async-done(((f32[16,32768]{1,0:T(8,128)}), f32[16,2048]{1,0:T(8,128)}) %reduce-scatter.5.cloned.1.call-update) | async-done | bytes 131088 | tf_op jit(solution)/shard_map/reduce_scatter | solution.py:84
  283.5 66.1 %all-reduce = (f32[16]{0:T(128)S(1)}, f32[16]{0:T(128)S(1)}) all-reduce(f32[16]{0:T(128)S(1)} %get-tuple-element.360, f32[16]{0:T(128)S(1)} %get-tuple-element.359), channel_id=1, replica_groups=mesh['row'=8,'col'=16] {'row','col'}, use_global_device_ids=true, to_apply=%region_1.2 | all-reduce | flops 32 | bytes 256 | tf_op jit(solution)/shard_map/psum | solution.py:62
  350.7 62.5 %psum.30 = f32[16]{0:T(128)S(1)} all-reduce(f32[16]{0:T(128)S(1)} %get-tuple-element.409), channel_id=1, replica_groups=mesh['row'=8,'col'=16] {'row','col'}, use_global_device_ids=true, to_apply=%region_12.13 | all-reduce | flops 16 | bytes 128 | tf_op jit(solution)/shard_map/psum | solution.py:62
  415.4 4.4 all-to-all-start.1
  420.4 26.2 %all-gather.5.cloned.1.call-done = f32[16,16384]{1,0:T(8,128)} async-done(((f32[16,2048]{1,0:T(8,128)}), f32[16,16384]{1,0:T(8,128)}) %all-gather.5.cloned.1.call-update) | async-done | bytes 1048592 | tf_op jit(solution)/shard_map/all_gather | solution.py:72
  458.1 96.3 %while.29 = (s32[]{:T(128)}, f32[16,128,256]{2,0,1:T(8,128)S(1)}, f32[16,64,256]{2,0,1:T(8,128)S(1)}, s32[4,12]{1,0:T(4,128)}, s32[4,12]{1,0:T(4,128)S(1)}, /*in...) while((s32[]{:T(128)}, f32[16,128,256]{2,0,1:T(8,128)S(1)}, ...), condition=%wide.region_17.18_spmd, body=%wide.region_13.17_spmd.sunk | while | flops 322635840 | bytes 12567965 | solution.py:83
  468.5 2.8 multiply_reduce_fusion.9
  471.3 3.9 fusion.93
  475.2 4.1 fusion.92
  495.3 3.9 fusion.93
  499.2 4.1 fusion.92
  519.4 3.9 fusion.93
  523.3 4.1 fusion.92
  540.7 2.8 multiply_reduce_fusion.9
  543.5 3.9 fusion.93
  547.4 4.1 fusion.92
  557.2 25.7 %reduce-scatter.11.cloned.1.call-done = f32[16,2048]{1,0:T(8,128)} async-done(((f32[16,16384]{1,0:T(8,128)}), f32[16,2048]{1,0:T(8,128)}) %reduce-scatter.11.cloned.1.call-update) | async-done | bytes 131088 | tf_op jit(solution)/shard_map/reduce_scatter | solution.py:90
  582.9 78.3 %reduce-scatter.9.cloned.1.call-done = f32[16,2048]{1,0:T(8,128)} async-done(((f32[16,32768]{1,0:T(8,128)}), f32[16,2048]{1,0:T(8,128)}) %reduce-scatter.9.cloned.1.call-update) | async-done | bytes 131088 | tf_op jit(solution)/shard_map/reduce_scatter | solution.py:84
  662.3 65.9 %psum.31 = f32[16]{0:T(128)S(1)} all-reduce(f32[16]{0:T(128)S(1)} %multiply_reduce_fusion.2), channel_id=1, replica_groups=mesh['row'=8,'col'=16] {'row','col'}, use_global_device_ids=true, to_apply=%region_21.22 | all-reduce | flops 16 | bytes 128 | tf_op jit(solution)/shard_map/psum | solution.py:97
  (205 shorter events, 163.1 us)
Async XLA Ops:
  7.2 11.7 %copy-start.13 = (s32[3,48]{1,0:T(4,128)S(1)}, s32[3,48]{1,0:T(4,128)}, u32[]{:S(2)}) copy-start(s32[3,48]{1,0:T(4,128)} %param.9) | copy-start | bytes 1732
  7.2 13.2 %copy-start.6 = (f32[3,2048]{1,0:T(4,128)S(1)}, f32[3,2048]{1,0:T(4,128)}, u32[]{:S(2)}) copy-start(f32[3,2048]{1,0:T(4,128)} %param.7) | copy-start | bytes 73732
  9.7 55.4 %all-to-all-start = ((f32[16,16,2048]{2,1,0:T(8,128)}), f32[16,16,2048]{2,1,0:T(8,128)S(1)}, u32[]{:S(2)}, u32[]{:S(2)}) async-start(f32[16,16,2048]{2,1,0:T(8,128)} %stack.4), calls=%async_computation | async-start | bytes 4194304 | tf_op jit(solution)/shard_map/all_to_all | solution.py:70
  18.1 44.6 %all-gather.3.cloned.1.call-start = ((), (), s32[]{:S(2)}) async-start(), calls=%async_computation.6 | async-start | bytes 1179648 | tf_op jit(solution)/shard_map/all_gather | solution.py:72
  18.8 185.1 %reduce-scatter.7.cloned.1.call-start = ((), (), s32[]{:S(2)}) async-start(), calls=%async_computation.8 | async-start | bytes 1179648 | tf_op jit(solution)/shard_map/reduce_scatter | solution.py:90
  82.6 2.8 copy-start.9
  85.5 3.9 copy-start.7
  106.7 2.8 copy-start.9
  109.5 3.9 copy-start.7
  130.8 2.8 copy-start.9
  133.6 3.9 copy-start.7
  154.9 2.8 copy-start.9
  157.7 3.9 copy-start.7
  169.7 112.6 %reduce-scatter.5.cloned.1.call-start = ((), (), s32[]{:S(2)}) async-start(), calls=%async_computation.7 | async-start | bytes 2228224 | tf_op jit(solution)/shard_map/reduce_scatter | solution.py:84
  169.8 112.6 %copy-start = (f32[16,2048]{1,0:T(8,128)S(1)}, f32[16,2048]{1,0:T(8,128)}, u32[]{:S(2)}) copy-start(f32[16,2048]{1,0:T(8,128)} %param.8) | copy-start | bytes 393220
  349.6 63.7 %copy-start.11 = (f32[16]{0:T(128)}, f32[16]{0:T(128)S(1)}, u32[]{:S(2)}) copy-start(f32[16]{0:T(128)S(1)} %div.31) | copy-start | bytes 196
  350.7 64.7 %copy-start.4 = (f32[16,2048]{1,0:T(8,128)}, f32[16,2048]{1,0:T(8,128)S(1)}, u32[]{:S(2)}) copy-start(f32[16,2048]{1,0:T(8,128)S(1)} %get-tuple-element.410) | copy-start | bytes 393220
  415.4 35.5 %all-to-all-start.1 = ((f32[16,16,2048]{2,1,0:T(8,128)}), f32[16,16,2048]{2,1,0:T(8,128)S(1)}, u32[]{:S(2)}, u32[]{:S(2)}) async-start(f32[16,16,2048]{2,1,0:T(8,128)} %stack.5), calls=%async_computation.3 | async-start | bytes 4194304 | tf_op jit(solution)/shard_map/all_to_all | solution.py:70
  419.8 26.8 %all-gather.5.cloned.1.call-start = ((), (), s32[]{:S(2)}) async-start(), calls=%async_computation.9 | async-start | bytes 1179648 | tf_op jit(solution)/shard_map/all_gather | solution.py:72
  420.4 162.5 %reduce-scatter.11.cloned.1.call-start = ((), (), s32[]{:S(2)}) async-start(), calls=%async_computation.11 | async-start | bytes 1179648 | tf_op jit(solution)/shard_map/reduce_scatter | solution.py:90
  468.4 2.8 copy-start.10
  471.3 3.9 copy-start.8
  495.3 3.9 copy-start.8
  519.4 3.9 copy-start.8
  540.7 2.8 copy-start.10
  543.5 3.9 copy-start.8
  555.5 105.6 %reduce-scatter.9.cloned.1.call-start = ((), (), s32[]{:S(2)}) async-start(), calls=%async_computation.10 | async-start | bytes 2228224 | tf_op jit(solution)/shard_map/reduce_scatter | solution.py:84
  555.6 105.6 %copy-start.3 = (f32[16,2048]{1,0:T(8,128)S(1)}, f32[16,2048]{1,0:T(8,128)}, u32[]{:S(2)}) copy-start(f32[16,2048]{1,0:T(8,128)} %copy-done.2) | copy-start | bytes 393220
  555.6 172.6 %copy-start.15 = (f32[16]{0:T(128)S(1)}, f32[16]{0:T(128)}, u32[]{:S(2)}) copy-start(f32[16]{0:T(128)} %copy-done.14) | copy-start | bytes 196
  555.6 172.6 %copy-start.1 = (f32[16,2048]{1,0:T(8,128)S(1)}, f32[16,2048]{1,0:T(8,128)}, u32[]{:S(2)}) copy-start(f32[16,2048]{1,0:T(8,128)} %param.8) | copy-start | bytes 393220
  555.6 172.6 %copy-start.5 = (f32[16,2048]{1,0:T(8,128)S(1)}, f32[16,2048]{1,0:T(8,128)}, u32[]{:S(2)}) copy-start(f32[16,2048]{1,0:T(8,128)} %copy-done.4) | copy-start | bytes 393220
  555.6 172.6 %copy-start.12 = (f32[16]{0:T(128)S(1)}, f32[16]{0:T(128)}, u32[]{:S(2)}) copy-start(f32[16]{0:T(128)} %copy-done.11) | copy-start | bytes 196
  (4 other events, 7.7 us)
Sparse Core Ops, SparseCore 0:
  20.6 25.6 all-gather.2
  169.8 34.0 reduce-scatter.6
  207.2 75.0 reduce-scatter.4
  422.6 23.9 all-gather.4
  555.6 27.2 reduce-scatter.10
  586.0 75.1 reduce-scatter.8
